TPU v7x, 512 devices: a whole 4x8x8 slice. The times are simulated.
512 devices in a mesh: row: 16 (over z, core), col: 32 (over y, x).
Axes of the slice: x: 4, y: 8, z: 8, core: 2. Of those that a mesh axis runs over, the one named last changes fastest.
Arguments:
- tokens: bfloat16 [4096, 2560], P('row', 'col'), may hold values from -6 to 6
- w_down: bfloat16 [2560, 1056], P('col'), may hold values from -0.125 to 0.125
- q_gain: float32 [768], replicated, may hold values from 0.1 to 1.9
- kv_gain: float32 [256], replicated, may hold values from 0.1 to 1.9
- w_q_up: bfloat16 [768, 3072], P(None, 'col'), may hold values from -8.8767604 to 8.8767604
- w_kv_up: bfloat16 [256, 4096], replicated, may hold values from -0.375 to 0.375
- w_out: bfloat16 [2048, 2560], P('col'), may hold values from -0.75 to 0.75
- latent_cache: bfloat16 [16, 8192, 288], P('row', 'col'), may hold values from -6 to 6
- cache_len: int32 [16], replicated, may hold values from 1 to 8192, as said below
- new_len: int32 [16], replicated, may hold values from 1 to 256, as said below
- page_table: int32 [16, 128], replicated, may hold values from 0 to 127, each once within a row
- home_slot: int32 [16], replicated, may hold values from 0 to 15, each once
Outputs:
- output: bfloat16 [4096, 2560], P('row', 'col')
Inputs may be any that keep to these rules, and one draw needn't show every extreme that they name: `cache_len`: some slot has exactly 8192 cached tokens; about half the slots hold at most 1024, the others at least 7168. `new_len`: some request has exactly 256 real new tokens.
All inputs are finite; a program needn't handle non-finite values.
Results may differ from a plain program's by a relative error of at most 0.023.
Values may be sent and summed in bfloat16 or wider, within the bound.
A program may use at most 64 MiB of HBM per device.

v0:
```python
import math
import jax
import jax.numpy as jnp
from jax import lax
from jax.sharding import PartitionSpec as P

NOPE = 64
ROPE = 32
VDIM = 64
epsilon = 1e-05


def rms_scale(values, gain):
    return values * lax.rsqrt(jnp.mean(values * values, axis=-1, keepdims=True) + epsilon) * gain


def angle_tables(positions, width):
    half_dim = width // 2
    frequency = 10000.0 ** (-2.0 * jnp.arange(half_dim, dtype=jnp.float32) / width)
    angles = positions.astype(jnp.float32)[:, None] * frequency[None, :]
    return (jnp.cos(angles), jnp.sin(angles))


def rotary(values, cosine, sine_table):
    half_dim = values.shape[-1] // 2
    first_half = values[..., :half_dim]
    second_half = values[..., half_dim:]
    return jnp.concatenate(
        [
            first_half * cosine - second_half * sine_table,
            second_half * cosine + first_half * sine_table,
        ],
        -1,
    )


def body(
    tokens,
    w_down,
    q_gain,
    kv_gain,
    w_q_up,
    w_kv_up,
    w_out,
    latent_cache,
    cache_len,
    new_len,
    page_table,
    home_slot,
):
    columns = lax.axis_size("col")
    column_id = lax.axis_index("col")
    row_id = lax.axis_index("row")
    group_rows = tokens.shape[0]
    own_rows = group_rows // columns
    q_width = q_gain.shape[0]
    kv_width = kv_gain.shape[0]
    slot_index = home_slot[row_id]
    cached_count = cache_len[slot_index]
    live_count = new_len[row_id]
    combined = lax.psum(jnp.dot(tokens, w_down, preferred_element_type=jnp.float32), "col")
    query_cos, query_sin = angle_tables(
        cached_count + jnp.arange(group_rows, dtype=jnp.int32), ROPE
    )
    query_latent = rms_scale(combined[:, :q_width], q_gain).astype(jnp.bfloat16)
    new_latent = rms_scale(combined[:, q_width : q_width + kv_width], kv_gain).astype(jnp.bfloat16)
    new_rope = rotary(combined[:, q_width + kv_width :], query_cos, query_sin).astype(jnp.bfloat16)
    fresh_latents = jnp.concatenate([new_latent, new_rope], 1)
    projected = jnp.dot(query_latent, w_q_up, preferred_element_type=jnp.float32)
    queries = jnp.concatenate(
        [projected[:, :NOPE], rotary(projected[:, NOPE:], query_cos, query_sin)], 1
    ).astype(jnp.bfloat16)
    segment = lax.all_gather(latent_cache, "row", axis=0, tiled=True)
    matches = jnp.arange(segment.shape[0], dtype=jnp.int32) == slot_index
    own_cache = jnp.sum(
        jnp.where(matches[:, None, None], segment.astype(jnp.float32), 0.0), 0
    ).astype(jnp.bfloat16)
    head_width = NOPE + VDIM
    head_weight = lax.dynamic_slice_in_dim(w_kv_up, column_id * head_width, head_width, 1)

    def expand(latents):
        lifted = jnp.dot(
            latents[:, :kv_width], head_weight, preferred_element_type=jnp.float32
        ).astype(jnp.bfloat16)
        return (jnp.concatenate([lifted[:, :NOPE], latents[:, kv_width:]], 1), lifted[:, NOPE:])

    cache_latents = lax.all_gather(own_cache, "col", axis=0, tiled=True)
    cache_keys, cache_values = expand(cache_latents)
    fresh_keys, fresh_values = expand(fresh_latents)
    key_total = cache_keys.shape[0]
    page_row = page_table[slot_index]
    page_count = page_row.shape[0]
    page_size = key_total // page_count
    block_size = min(512, key_total)
    offsets = jnp.arange(page_size, dtype=jnp.int32)
    page_ids = jnp.arange(page_count, dtype=jnp.int32)
    logical_page = jnp.sum(
        page_ids[:, None] * (page_row[:, None] == page_ids[None, :]).astype(jnp.int32), 0
    )
    cached_visible = (logical_page[:, None] * page_size + offsets[None, :]).reshape(
        key_total
    ) < cached_count
    block_limit = key_total // block_size
    score_scale = 1.0 / math.sqrt(NOPE + ROPE)
    query_index = jnp.arange(group_rows, dtype=jnp.int32)[:, None]
    key_index = jnp.arange(group_rows, dtype=jnp.int32)[None, :]
    fresh_visible = (key_index <= query_index) & (key_index < live_count)
    fresh_scores = (
        jnp.einsum("qd,kd->qk", queries, fresh_keys, preferred_element_type=jnp.float32)
        * score_scale
    )
    fresh_scores = jnp.where(fresh_visible, fresh_scores, -jnp.inf)
    first_peak = jnp.max(fresh_scores, 1)
    fresh_exponent = jnp.exp(fresh_scores - first_peak[:, None])
    start_state = (
        first_peak,
        jnp.sum(fresh_exponent, 1),
        jnp.dot(
            fresh_exponent.astype(jnp.bfloat16), fresh_values, preferred_element_type=jnp.float32
        ),
    )

    def accumulate(block_id, running):
        row_peak, row_total, summed = running
        key_block = lax.dynamic_slice_in_dim(cache_keys, block_id * block_size, block_size, 0)
        mask_block = lax.dynamic_slice_in_dim(cached_visible, block_id * block_size, block_size, 0)
        value_block = lax.dynamic_slice_in_dim(cache_values, block_id * block_size, block_size, 0)
        raw_scores = (
            jnp.einsum("qd,kd->qk", queries, key_block, preferred_element_type=jnp.float32)
            * score_scale
        )
        raw_scores = jnp.where(mask_block[None, :], raw_scores, -jnp.inf)
        next_peak = jnp.maximum(row_peak, jnp.max(raw_scores, 1))
        factor = jnp.exp(row_peak - next_peak)
        exponent = jnp.exp(raw_scores - next_peak[:, None])
        next_total = row_total * factor + jnp.sum(exponent, 1)
        next_summed = summed * factor[:, None] + jnp.dot(
            exponent.astype(jnp.bfloat16), value_block, preferred_element_type=jnp.float32
        )
        return (next_peak, next_total, next_summed)

    row_peak, row_total, summed = lax.fori_loop(0, block_limit, accumulate, start_state)
    attended = (summed / row_total[:, None]).astype(jnp.bfloat16)
    live_rows = jnp.arange(group_rows, dtype=jnp.int32) < live_count
    attended = jnp.where(live_rows[:, None], attended, jnp.zeros_like(attended))
    summed_out = lax.psum_scatter(
        lax.dot_general(
            w_out, attended, (((0,), (1,)), ((), ())), preferred_element_type=jnp.float32
        ).astype(jnp.bfloat16),
        "col",
        scatter_dimension=0,
        tiled=True,
    ).astype(jnp.float32)
    result = summed_out.T.astype(jnp.bfloat16)
    return result


def solution(mesh):
    return jax.shard_map(
        body,
        mesh=mesh,
        in_specs=(
            P("row", "col"),
            P("col", None),
            P(),
            P(),
            P(None, "col"),
            P(),
            P("col", None),
            P("row", "col", None),
            P(),
            P(),
            P(),
            P(),
        ),
        out_specs=P("row", "col"),
        check_vma=False,
    )
```

profile of v0, /device:TPU:16, one launch (start us, length us, event | category | flops | bytes accessed | tf_op | source)
XLA Modules:
  0.0 532.0 jit_solution(8802280258935113749)
XLA Ops:
  7.4 0.7 all-gather.3.cloned.1.call-update
  8.1 2.3 fusion.57
  10.6 0.6 dynamic_slice.37
  11.2 0.6 iota_compare_fusion.3
  11.8 46.3 %all-gather.3.cloned.1.call-done = bf16[16,256,288]{1,2,0:T(8,128)(2,1)} async-done(((bf16[1,256,288]{1,2,0:T(8,128)(2,1)}), bf16[16,256,288]{1,2,0:T(8,128)(2,1)}) %all-gather.3.cloned.1.call-update) | async-done | bytes 2359312 | tf_op jit(solution)/shard_map/all_gather | solution.py:73
  58.2 2.9 select_reduce_fusion
  62.4 0.6 dynamic_slice.36
  63.7 0.6 dynamic_slice.38
  64.3 0.7 dynamic-slice_bitcast_fusion
  65.1 0.7 add_compare_fusion
  66.0 0.6 iota_compare_fusion.2
  66.6 0.6 add_convert_fusion
  67.2 109.0 %all-reduce.2.cloned.1.call-done = f32[256,1056]{0,1:T(8,128)} async-done(((f32[256,1056]{0,1:T(8,128)}), f32[256,1056]{0,1:T(8,128)}) %all-reduce.2.cloned.1.call-update) | async-done | bytes 1081360 | tf_op jit(solution)/shard_map/psum | solution.py:61
  176.2 1.0 multiply_reduce_fusion.1
  177.3 1.2 convolution_convert_fusion.2
  178.5 1.3 multiply_reduce_fusion
  179.8 1.4 fusion.12
  181.2 0.9 fusion.42
  182.2 0.3 fusion.56
  182.6 0.2 fusion.18
  182.7 84.2 %all-gather.5.cloned.1.call-done = bf16[8192,288]{0,1:T(8,128)(2,1)} async-done(((bf16[256,288]{0,1:T(8,128)(2,1)}), bf16[8192,288]{0,1:T(8,128)(2,1)}) %all-gather.5.cloned.1.call-update) | async-done | bytes 4718608 | tf_op jit(solution)/shard_map/all_gather | solution.py:87
  266.9 2.9 convolution_convert_fusion
  269.9 0.1 fusion.55
  270.1 0.9 slice-done
  270.9 1.3 pad_maximum_fusion
  272.2 26.9 %while.17 = (s32[]{:T(128)}, f32[256]{0:T(256)S(1)}, f32[256]{0:T(256)S(1)}, f32[256,64]{0,1:T(8,128)S(1)}, pred[8192]{0:T(1024)(128)(4,1)S(1)}, /*index=5*/bf16...) while((s32[]{:T(128)}, f32[256]{0:T(256)S(1)}, ...), condition=%wide.region_10.11_spmd, body=%wide.region_7.10_spmd.sunk | while | flops 42893828 | bytes 1935023 | solution.py:142
  272.3 1.2 fusion.71
  273.5 0.1 fusion.72
  273.6 0.2 convolution_add_fusion.2
  273.9 1.2 fusion.71
  275.1 0.1 fusion.72
  275.3 0.2 convolution_add_fusion.2
  275.6 1.2 fusion.71
  276.8 0.1 fusion.72
  277.0 0.2 convolution_add_fusion.2
  277.3 1.2 fusion.71
  278.6 0.2 convolution_add_fusion.2
  279.0 1.2 fusion.71
  280.3 0.2 convolution_add_fusion.2
  280.7 1.2 fusion.71
  282.0 0.2 convolution_add_fusion.2
  282.4 1.2 fusion.71
  283.7 0.2 convolution_add_fusion.2
  284.1 1.2 fusion.71
  285.4 0.2 convolution_add_fusion.2
  285.7 1.2 fusion.71
  287.1 0.2 convolution_add_fusion.2
  287.4 1.2 fusion.71
  288.8 0.2 convolution_add_fusion.2
  289.1 1.2 fusion.71
  290.4 0.2 convolution_add_fusion.2
  290.8 1.2 fusion.71
  292.1 0.2 convolution_add_fusion.2
  292.5 1.2 fusion.71
  293.8 0.2 convolution_add_fusion.2
  294.2 1.2 fusion.71
  295.5 0.2 convolution_add_fusion.2
  295.8 1.2 fusion.71
  297.2 0.2 convolution_add_fusion.2
  297.5 1.2 fusion.71
  298.9 0.2 convolution_add_fusion.2
  299.1 1.5 fusion.10
  300.6 1.5 copy.29
  302.1 222.3 %reduce-scatter.4.cloned.1.call-done = bf16[80,256]{1,0:T(8,128)(2,1)} async-done(((bf16[2560,256]{1,0:T(8,128)(2,1)}), bf16[80,256]{1,0:T(8,128)(2,1)}) %reduce-scatter.4.cloned.1.call-update) | async-done | bytes 40976
  (110 shorter events, 3.9 us)
Async XLA Ops:
  7.4 169.9 %copy-start = (bf16[256,4096]{1,0:T(8,128)(2,1)S(1)}, bf16[256,4096]{1,0:T(8,128)(2,1)}, u32[]{:S(2)}) copy-start(bf16[256,4096]{1,0:T(8,128)(2,1)} %param.19) | copy-start | bytes 6291460
  7.4 3.2 copy-start.4
  7.4 50.8 %all-gather.3.cloned.1.call-start = ((), (), s32[]{:S(2)}) async-start(), calls=%async_computation.2 | async-start | bytes 2506752 | tf_op jit(solution)/shard_map/all_gather | solution.py:73
  8.1 168.1 %all-reduce.2.cloned.1.call-start = ((), (), s32[]{:S(2)}) async-start(), calls=%async_computation.1 | async-start | bytes 2162688 | tf_op jit(solution)/shard_map/psum | solution.py:61
  10.5 52.0 %copy-start.5 = (s32[16]{0:T(128)S(1)}, s32[16]{0:T(128)}, u32[]{:S(2)}) copy-start(s32[16]{0:T(128)} %param.23) | copy-start | bytes 196
  10.5 53.3 %copy-start.6 = (s32[16]{0:T(128)S(1)}, s32[16]{0:T(128)}, u32[]{:S(2)}) copy-start(s32[16]{0:T(128)} %param.22) | copy-start | bytes 196
  10.5 166.8 %copy-start.3 = (f32[256]{0:T(256)S(1)}, f32[256]{0:T(256)}, u32[]{:S(2)}) copy-start(f32[256]{0:T(256)} %param.17) | copy-start | bytes 3076
  10.5 256.4 %all-gather.5.cloned.1.call-start = ((), (), s32[]{:S(2)}) async-start(), calls=%async_computation.3 | async-start | bytes 4866048 | tf_op jit(solution)/shard_map/all_gather | solution.py:87
  11.8 167.9 %copy-start.1 = (bf16[768,96]{0,1:T(8,128)(2,1)S(1)}, bf16[768,96]{0,1:T(8,128)(2,1)}, u32[]{:S(2)}) copy-start(bf16[768,96]{0,1:T(8,128)(2,1)} %param.18) | copy-start | bytes 442372
  11.8 167.9 %copy-start.2 = (f32[768]{0:T(1024)S(1)}, f32[768]{0:T(1024)}, u32[]{:S(2)}) copy-start(f32[768]{0:T(1024)} %param.16) | copy-start | bytes 9220
  61.1 463.3 %reduce-scatter.4.cloned.1.call-start = ((), (), s32[]{:S(2)}) async-start(), calls=%async_computation.4 | async-start | bytes 1351680
  269.9 1.0 slice-start
Sparse Core Ops, SparseCore 0:
  10.3 47.8 all-gather.2
Sparse Core Ops, SparseCore 1:
  12.0 164.2 all-reduce.1
  179.2 87.7 all-gather.4
  302.2 222.2 reduce-scatter.3
where the time goes:
time: 533 us; the launch traced here: 532 us
  waiting for transfers between devices  463 us (87%)
  matrix products  32.4 us (6%)
  between operations  17.1 us (3%)
  other arithmetic  12.4 us (2%)
  local copies, waits for them, and re-layouts  6.62 us (1%)
    unnamed x5, waiting for transfers between devices  223 us
    psum x1, waiting for transfers between devices, body(): lax.psum(jnp.dot(tokens, w_down, preferred_element_type=jnp.float32), 'col')  109 us
    all_gather x1, waiting for transfers between devices, body(): cache_latents = lax.all_gather(own_cache, 'col', axis=0, tiled=True)  84.2 us
    all_gather x1, waiting for transfers between devices, body(): segment = lax.all_gather(latent_cache, 'row', axis=0, tiled=True)  46.3 us
    dot_general x16, matrix products, accumulate(): jnp.einsum('qd,kd->qk', queries, key_block, preferred_element_type=jnp.fl...  18.8 us
  transfers between devices with their start and end apart: 4, of which 4 were waited for; matrix products, arithmetic and copies ran while one was open for 3% of the time, Pallas kernels for 0%

commit v1 on v0

--- a/solution.py
+++ b/solution.py
@@ -58,7 +58,9 @@
     slot_index = home_slot[row_id]
     cached_count = cache_len[slot_index]
     live_count = new_len[row_id]
-    combined = lax.psum(jnp.dot(tokens, w_down, preferred_element_type=jnp.float32), "col")
+    combined = jnp.sum(
+        lax.all_gather(jnp.dot(tokens, w_down, preferred_element_type=jnp.float32), "col"), axis=0
+    )
     query_cos, query_sin = angle_tables(
         cached_count + jnp.arange(group_rows, dtype=jnp.int32), ROPE
     )

time: 533 us -> 691 us (1.30)
  waiting for transfers between devices: 463 us -> 602 us
  local copies, waits for them, and re-layouts: 6.62 us -> 27.7 us
    all_gather x0 -> x1, waiting for transfers between devices: none -> 254 us  [body(): lax.all_gather(jnp.dot(tokens, w_down, preferred_element_type=jnp.float32...]
    psum x1 -> x0, waiting for transfers between devices: 109 us -> none  [body(): lax.psum(jnp.dot(tokens, w_down, preferred_element_type=jnp.float32), 'col')]
    unnamed x15 -> x18, local copies, waits for them, and re-layouts: 1.49 us -> 22 us
  transfers between devices with their start and end apart: 4 -> 4, of which waited for: 4 -> 4; matrix products, arithmetic and copies ran while one was open for 3% -> 2% of each run, Pallas kernels for 0% -> 0%
where the time goes in v1:
time: 691 us; the launch traced here: 690 us
  waiting for transfers between devices  602 us (87%)
  matrix products  29.3 us (4%)
  local copies, waits for them, and re-layouts  27.7 us (4%)
  other arithmetic  15.1 us (2%)
  between operations  15.1 us (2%)
    all_gather x1, waiting for transfers between devices, body(): lax.all_gather(jnp.dot(tokens, w_down, preferred_element_type=jnp.float32...  254 us
    unnamed x5, waiting for transfers between devices  219 us
    all_gather x1, waiting for transfers between devices, body(): cache_latents = lax.all_gather(own_cache, 'col', axis=0, tiled=True)  80.3 us
    all_gather x1, waiting for transfers between devices, body(): segment = lax.all_gather(latent_cache, 'row', axis=0, tiled=True)  48.2 us
    unnamed x18, local copies, waits for them, and re-layouts  22 us
    dot_general x16, matrix products, accumulate(): jnp.einsum('qd,kd->qk', queries, key_block, preferred_element_type=jnp.fl...  18.7 us
  transfers between devices with their start and end apart: 4, of which 4 were waited for; matrix products, arithmetic and copies ran while one was open for 2% of the time, Pallas kernels for 0%

profile of v1, /device:TPU:16, one launch (start us, length us, event | category | flops | bytes accessed | tf_op | source)
XLA Modules:
  0.0 690.0 jit_solution(6567342313598170820)
XLA Ops:
  6.5 0.7 all-gather.5.cloned.1.call-update
  7.3 1.2 dynamic_slice.37
  8.6 0.6 iota_compare_fusion.3
  9.2 48.2 %all-gather.5.cloned.1.call-done = bf16[16,256,288]{1,2,0:T(8,128)(2,1)} async-done(((bf16[1,256,288]{1,2,0:T(8,128)(2,1)}), bf16[16,256,288]{1,2,0:T(8,128)(2,1)}) %all-gather.5.cloned.1.call-update) | async-done | bytes 2359312 | tf_op jit(solution)/shard_map/all_gather | solution.py:75
  57.4 2.9 select_reduce_fusion
  60.4 1.3 fusion.57
  62.9 0.6 dynamic_slice.36
  64.1 0.6 dynamic_slice.38
  64.7 0.7 dynamic-slice_bitcast_fusion
  65.5 0.7 add_compare_fusion
  66.3 0.6 iota_compare_fusion.2
  67.0 0.6 add_convert_fusion
  67.5 80.3 %all-gather.7.cloned.1.call-done = bf16[8192,288]{0,1:T(8,128)(2,1)} async-done(((bf16[256,288]{0,1:T(8,128)(2,1)}), bf16[8192,288]{0,1:T(8,128)(2,1)}) %all-gather.7.cloned.1.call-update) | async-done | bytes 4718608 | tf_op jit(solution)/shard_map/all_gather | solution.py:89
  147.8 2.9 convolution_convert_fusion
  150.8 0.1 fusion.55
  150.9 0.9 slice-done
  151.8 1.2 pad_maximum_fusion
  153.1 254.5 %all-gather.9.cloned.1.call-done = f32[8192,1056]{0,1:T(8,128)} async-done(((f32[256,1056]{0,1:T(8,128)}), f32[8192,1056]{0,1:T(8,128)}) %all-gather.9.cloned.1.call-update) | async-done | bytes 34603024 | tf_op jit(solution)/shard_map/all_gather | solution.py:62
  407.5 20.5 %copy.34 = f32[132,8,32,256]{3,2,1,0:T(8,128)S(1)} copy(f32[132,8,32,256]{3,1,2,0:T(8,128)} %bitcast.22) | data formatting | bytes 69206016
  428.0 5.7 bitcast_reduce_fusion
  433.9 0.3 convolution_convert_fusion.2
  434.2 0.3 fusion.12
  434.6 0.1 fusion.42
  434.7 0.3 fusion.56
  435.0 0.2 fusion.18
  435.3 26.7 %while.17 = (s32[]{:T(128)}, f32[256]{0:T(256)S(1)}, f32[256]{0:T(256)S(1)}, f32[256,64]{0,1:T(8,128)S(1)}, pred[8192]{0:T(1024)(128)(4,1)S(1)}, /*index=5*/bf16...) while((s32[]{:T(128)}, f32[256]{0:T(256)S(1)}, ...), condition=%wide.region_10.11_spmd, body=%wide.region_7.10_spmd.sunk | while | flops 42893828 | bytes 1935031 | solution.py:144
  435.4 1.2 fusion.71
  436.6 0.1 fusion.72
  436.8 0.2 convolution_add_fusion.2
  437.1 1.2 fusion.71
  438.4 0.2 convolution_add_fusion.2
  438.8 1.2 fusion.71
  440.0 0.1 fusion.72
  440.1 0.2 convolution_add_fusion.2
  440.5 1.2 fusion.71
  441.8 0.2 convolution_add_fusion.2
  442.1 1.2 fusion.71
  443.5 0.2 convolution_add_fusion.2
  443.8 1.2 fusion.71
  445.1 0.2 convolution_add_fusion.2
  445.5 1.2 fusion.71
  446.8 0.2 convolution_add_fusion.2
  447.1 1.2 fusion.71
  448.3 0.1 fusion.72
  448.5 0.2 convolution_add_fusion.2
  448.8 1.2 fusion.71
  450.1 0.2 convolution_add_fusion.2
  450.5 1.2 fusion.71
  451.8 0.2 convolution_add_fusion.2
  452.2 1.2 fusion.71
  453.5 0.2 convolution_add_fusion.2
  453.8 1.2 fusion.71
  455.2 0.2 convolution_add_fusion.2
  455.5 1.2 fusion.71
  456.8 0.2 convolution_add_fusion.2
  457.2 1.2 fusion.71
  458.5 0.2 convolution_add_fusion.2
  458.8 1.2 fusion.71
  460.2 0.2 convolution_add_fusion.2
  460.5 1.2 fusion.71
  461.9 0.2 convolution_add_fusion.2
  462.1 1.5 fusion.10
  463.6 1.5 copy.29
  465.1 218.4 %reduce-scatter.4.cloned.1.call-done = bf16[80,256]{1,0:T(8,128)(2,1)} async-done(((bf16[2560,256]{1,0:T(8,128)(2,1)}), bf16[80,256]{1,0:T(8,128)(2,1)}) %reduce-scatter.4.cloned.1.call-update) | async-done | bytes 40976
  (114 shorter events, 4.1 us)
Async XLA Ops:
  6.5 141.3 %copy-start = (bf16[256,4096]{1,0:T(8,128)(2,1)S(1)}, bf16[256,4096]{1,0:T(8,128)(2,1)}, u32[]{:S(2)}) copy-start(bf16[256,4096]{1,0:T(8,128)(2,1)} %param.19) | copy-start | bytes 6291460
  6.5 53.8 %copy-start.3 = (bf16[256,80]{0,1:T(8,128)(2,1)S(1)}, bf16[256,80]{0,1:T(8,128)(2,1)}, u32[]{:S(2)}) copy-start(bf16[256,80]{0,1:T(8,128)(2,1)} %param.14) | copy-start | bytes 122884
  6.5 53.8 %copy-start.1 = (bf16[80,1056]{1,0:T(8,128)(2,1)S(1)}, bf16[80,1056]{1,0:T(8,128)(2,1)}, u32[]{:S(2)}) copy-start(bf16[80,1056]{1,0:T(8,128)(2,1)} %param.15) | copy-start | bytes 506884
  6.5 50.8 %all-gather.5.cloned.1.call-start = ((), (), s32[]{:S(2)}) async-start(), calls=%async_computation.1 | async-start | bytes 2506752 | tf_op jit(solution)/shard_map/all_gather | solution.py:75
  7.3 140.6 %all-gather.7.cloned.1.call-start = ((), (), s32[]{:S(2)}) async-start(), calls=%async_computation.2 | async-start | bytes 4866048 | tf_op jit(solution)/shard_map/all_gather | solution.py:89
  9.1 53.8 %copy-start.6 = (s32[16]{0:T(128)S(1)}, s32[16]{0:T(128)}, u32[]{:S(2)}) copy-start(s32[16]{0:T(128)} %param.23) | copy-start | bytes 196
  9.2 55.0 %copy-start.7 = (s32[16]{0:T(128)S(1)}, s32[16]{0:T(128)}, u32[]{:S(2)}) copy-start(s32[16]{0:T(128)} %param.22) | copy-start | bytes 196
  60.3 347.3 %all-gather.9.cloned.1.call-start = ((), (), s32[]{:S(2)}) async-start(), calls=%async_computation.3 | async-start | bytes 35684352 | tf_op jit(solution)/shard_map/all_gather | solution.py:62
  61.7 621.8 %reduce-scatter.4.cloned.1.call-start = ((), (), s32[]{:S(2)}) async-start(), calls=%async_computation.4 | async-start | bytes 1351680
  150.8 1.0 slice-start
  428.0 5.9 copy-start.5
  428.0 6.2 copy-start.2
  428.0 6.2 copy-start.4
Sparse Core Ops, SparseCore 0:
  9.5 47.8 all-gather.4
  60.4 87.3 all-gather.6
  150.9 256.6 all-gather.8
  465.2 218.2 reduce-scatter.3
